TPU v7x, 128 devices: a whole 4x4x4 slice. The times are simulated.
128 devices in a mesh: box: 128 (over x, y, z, core).
Axes of the slice: x: 4, y: 4, z: 4, core: 2. Of those that a mesh axis runs over, the one named last changes fastest.
Arguments:
- sources: float32 [2048, 131072], P(None, 'box'), may hold values from -6 to 6
- leaf_basis: bfloat16 [256, 512, 256], P('box'), may hold values from -0.25 to 0.25
- stay_blocks: bfloat16 [8, 256, 256, 256], P(None, 'box'), may hold values from -0.25 to 0.25
- cross_blocks: bfloat16 [8, 256, 256, 256], P(None, 'box'), may hold values from -0.25 to 0.25
- out_basis: bfloat16 [256, 256, 512], P('box'), may hold values from -0.375 to 0.375
- near_blocks: bfloat16 [256, 768, 512], P('box'), may hold values from -0.21875 to 0.21875
Outputs:
- targets: float32 [2048, 131072], P(None, 'box')
All inputs are finite; a program needn't handle non-finite values.
Results may differ from a plain program's by a relative error of at most 0.014.
Values may be sent and summed in bfloat16 or wider, within the bound.
A program may use at most 128 MiB of HBM per device.

v0:
```python
import jax
import jax.numpy as jnp
from jax import lax
from jax.sharding import PartitionSpec as P

B = 512
H = 128


def with_halo(cells, sides, width):
    for axis, dim in sides:
        count = lax.axis_size(axis)
        ends = count - 1
        head = lax.slice_in_dim(cells, 0, width, axis=dim)
        tail = lax.slice_in_dim(cells, cells.shape[dim] - width, cells.shape[dim], axis=dim)
        cells = jnp.concatenate(
            [
                lax.ppermute(tail, axis, [(i, (i + 1) % count) for i in range(ends)]),
                cells,
                lax.ppermute(head, axis, [((i + 1) % count, i) for i in range(ends)]),
            ],
            axis=dim,
        )
    return cells


def from_partner(shard, axis, apart):
    return lax.ppermute(shard, axis, [(i, i ^ 1 << apart) for i in range(lax.axis_size(axis))])


def near_terms(rounded, near_blocks):
    padded = with_halo(rounded, (("box", 1),), H)
    return [
        jnp.dot(
            padded[:, which * B : which * B + B + 2 * H],
            near_blocks[which],
            preferred_element_type=jnp.float32,
        )
        for which in range(2)
    ]


def per_device(sources, leaf_basis, stay_blocks, cross_blocks, out_basis, near_blocks):
    rounded = sources.astype(jnp.bfloat16)
    proxies = [
        jnp.dot(
            rounded[:, which * B : (which + 1) * B],
            leaf_basis[which],
            preferred_element_type=jnp.float32,
        ).astype(jnp.bfloat16)
        for which in range(2)
    ]
    first = jnp.dot(proxies[0], stay_blocks[0, 0], preferred_element_type=jnp.float32) + jnp.dot(
        proxies[1], cross_blocks[0, 1], preferred_element_type=jnp.float32
    )
    second = jnp.dot(proxies[1], stay_blocks[0, 1], preferred_element_type=jnp.float32) + jnp.dot(
        proxies[0], cross_blocks[0, 0], preferred_element_type=jnp.float32
    )
    proxies = [first.astype(jnp.bfloat16), second.astype(jnp.bfloat16)]
    depths = stay_blocks.shape[0]
    for depth_at in range(1, depths):
        moved = from_partner(
            (
                jnp.dot(proxies[0], cross_blocks[depth_at, 0], preferred_element_type=jnp.float32),
                jnp.dot(proxies[1], cross_blocks[depth_at, 1], preferred_element_type=jnp.float32),
            ),
            "box",
            depth_at - 1,
        )
        proxies = [
            (
                jnp.dot(
                    proxies[which], stay_blocks[depth_at, which], preferred_element_type=jnp.float32
                )
                + moved[which]
            ).astype(jnp.bfloat16)
            for which in range(2)
        ]
    near_field = near_terms(rounded, near_blocks)
    columns = [
        jnp.dot(proxies[which], out_basis[which], preferred_element_type=jnp.float32)
        + near_field[which]
        for which in range(2)
    ]
    return jnp.concatenate(columns, axis=1)


def solution(mesh):
    in_specs = (
        P(None, "box"),
        P("box", None, None),
        P(None, "box", None, None),
        P(None, "box", None, None),
        P("box", None, None),
        P("box", None, None),
    )
    out_specs = P(None, "box")
    return jax.shard_map(
        per_device, mesh=mesh, in_specs=in_specs, out_specs=out_specs, check_vma=False
    )
```

profile of v0, /device:TPU:123, one launch (start us, length us, event | category | flops | bytes accessed | tf_op | source)
XLA Modules:
  0.0 524.9 jit_solution(1235591390810039671)
XLA Ops:
  0.0 4.1 convert_element_type.57
  5.5 1.3 fusion.57
  6.9 1.3 fusion.12
  8.2 1.3 fusion.53
  11.7 1.3 fusion.4
  13.0 1.3 fusion.78
  14.5 1.3 fusion.13
  15.8 1.3 fusion.50
  18.6 1.3 fusion.5
  19.9 1.3 fusion.75
  21.5 42.5 %collective-permute-done.9 = f32[2048,256]{1,0:T(8,128)S(1)} collective-permute-done((f32[2048,256]{1,0:T(8,128)S(1)}, f32[2048,256]{1,0:T(8,128)S(1)}, u32[]{:S(2)}, u32[]{:S(2)}) %collective-permute-start.9) | collective-permute-done | bytes 2097184 | tf_op jit(solution)/shard_map/ppermute | solution.py:28
  63.9 1.3 fusion.14
  65.3 1.3 fusion.47
  66.9 41.9 %collective-permute-done.1 = f32[2048,256]{1,0:T(8,128)S(1)} collective-permute-done((f32[2048,256]{1,0:T(8,128)S(1)}, f32[2048,256]{1,0:T(8,128)S(1)}, u32[]{:S(2)}, u32[]{:S(2)}) %collective-permute-start.1) | collective-permute-done | bytes 2097184 | tf_op jit(solution)/shard_map/ppermute | solution.py:28
  108.9 1.3 fusion.6
  110.2 1.3 fusion.72
  111.9 40.9 %collective-permute-done.10 = f32[2048,256]{1,0:T(8,128)S(1)} collective-permute-done((f32[2048,256]{1,0:T(8,128)S(1)}, f32[2048,256]{1,0:T(8,128)S(1)}, u32[]{:S(2)}, u32[]{:S(2)}) %collective-permute-start.10) | collective-permute-done | bytes 2097184 | tf_op jit(solution)/shard_map/ppermute | solution.py:28
  152.8 1.3 fusion.15
  154.1 1.3 fusion.44
  156.0 41.7 %collective-permute-done.2 = f32[2048,256]{1,0:T(8,128)S(1)} collective-permute-done((f32[2048,256]{1,0:T(8,128)S(1)}, f32[2048,256]{1,0:T(8,128)S(1)}, u32[]{:S(2)}, u32[]{:S(2)}) %collective-permute-start.2) | collective-permute-done | bytes 2097184 | tf_op jit(solution)/shard_map/ppermute | solution.py:28
  199.0 1.3 fusion.69
  200.9 1.3 fusion.16
  202.3 1.3 fusion.41
  204.5 42.0 %collective-permute-done.3 = f32[2048,256]{1,0:T(8,128)S(1)} collective-permute-done((f32[2048,256]{1,0:T(8,128)S(1)}, f32[2048,256]{1,0:T(8,128)S(1)}, u32[]{:S(2)}, u32[]{:S(2)}) %collective-permute-start.3) | collective-permute-done | bytes 2097184 | tf_op jit(solution)/shard_map/ppermute | solution.py:28
  246.5 1.3 fusion.8
  247.8 1.3 fusion.66
  250.4 40.7 %collective-permute-done.12 = f32[2048,256]{1,0:T(8,128)S(1)} collective-permute-done((f32[2048,256]{1,0:T(8,128)S(1)}, f32[2048,256]{1,0:T(8,128)S(1)}, u32[]{:S(2)}, u32[]{:S(2)}) %collective-permute-start.12) | collective-permute-done | bytes 2097184 | tf_op jit(solution)/shard_map/ppermute | solution.py:28
  291.1 1.3 fusion.17
  292.5 1.3 fusion.38
  294.4 41.7 %collective-permute-done.4 = f32[2048,256]{1,0:T(8,128)S(1)} collective-permute-done((f32[2048,256]{1,0:T(8,128)S(1)}, f32[2048,256]{1,0:T(8,128)S(1)}, u32[]{:S(2)}, u32[]{:S(2)}) %collective-permute-start.4) | collective-permute-done | bytes 2097184 | tf_op jit(solution)/shard_map/ppermute | solution.py:28
  336.1 1.3 fusion.9
  337.4 1.3 fusion.63
  339.3 1.3 fusion.18
  340.6 1.3 fusion.34
  342.0 2.0 collective-permute-start.14
  344.0 40.0 %collective-permute-done.5 = f32[2048,256]{1,0:T(8,128)S(1)} collective-permute-done((f32[2048,256]{1,0:T(8,128)S(1)}, f32[2048,256]{1,0:T(8,128)S(1)}, u32[]{:S(2)}, u32[]{:S(2)}) %collective-permute-start.5) | collective-permute-done | bytes 2097184 | tf_op jit(solution)/shard_map/ppermute | solution.py:28
  384.0 1.3 fusion.10
  385.4 2.8 fusion.59
  388.2 1.8 collective-permute-start.6
  390.2 7.5 %collective-permute-start.15 = (bf16[2048,128]{1,0:T(8,128)(2,1)S(1)}, bf16[2048,128]{1,0:T(8,128)(2,1)S(1)}, u32[]{:S(2)}, u32[]{:S(2)}) collective-permute-start(bf16[2048,128]{1,0:T(8,128)(2,1)S(1)} %get-tuple-element.6), channel_id=1, source_target_pairs={{1,0},{2,1},{3,2},{4,3},{5,4},{6,5},{7,6},{8,7},{9,8},{10,9},{11,1... | collective-permute-start | bytes 1572872 | tf_op jit(solution)/shard_map/ppermute | solution.py:20
  397.7 7.0 %collective-permute-start.7 = (bf16[2048,128]{1,0:T(8,128)(2,1)S(1)}, bf16[2048,128]{1,0:T(8,128)(2,1)S(1)}, u32[]{:S(2)}, u32[]{:S(2)}) collective-permute-start(bf16[2048,128]{1,0:T(8,128)(2,1)S(1)} %get-tuple-element.5), channel_id=1, source_target_pairs={{0,1},{1,2},{2,3},{3,4},{4,5},{5,6},{6,7},{7,8},{8,9},{9,10},{10,1... | collective-permute-start | bytes 1572872 | tf_op jit(solution)/shard_map/ppermute | solution.py:18
  404.7 83.3 %collective-permute-done.15 = bf16[2048,128]{1,0:T(8,128)(2,1)S(1)} collective-permute-done((bf16[2048,128]{1,0:T(8,128)(2,1)S(1)}, bf16[2048,128]{1,0:T(8,128)(2,1)S(1)}, u32[]{:S(2)}, u32[]{:S(2)}) %collective-permute-start.15) | collective-permute-done | bytes 524320 | tf_op jit(solution)/shard_map/ppermute | solution.py:20
  488.0 3.9 fusion
  492.0 3.9 fusion.2
  495.9 6.0 %convolution_add_fusion = f32[2048,512]{0,1:T(8,128)} fusion(f32[2048,512]{0,1:T(8,128)} %fusion, f32[2048,256]{1,0:T(8,128)} %collective-permute-done.14, bf16[2048,256]{1,0:T(8,128)(2,1)S(1)} %fusion.18, bf16[2,256,512]{2,1,0:T(8,128)(2,1)S(1)} %copy-done, bf16[8,2,256,256]{3,2,1,0:T(8,128)(2,1)} %param.8), kind=kOutput, calls=%fused_computation.1 | convolution fusion | flops 807403520 | bytes 11927552 | tf_op jit(solution)/shard_map/dot_general | solution.py:81
  501.9 6.0 %convolution_add_fusion.1 = f32[2048,512]{0,1:T(8,128)} fusion(f32[2048,512]{0,1:T(8,128)} %fusion.2, f32[2048,256]{1,0:T(8,128)} %collective-permute-done.6, bf16[2048,256]{1,0:T(8,128)(2,1)S(1)} %fusion.10, bf16[2,256,512]{2,1,0:T(8,128)(2,1)S(1)} %copy-done, bf16[8,2,256,256]{3,2,1,0:T(8,128)(2,1)} %param.8), kind=kOutput, calls=%fused_computation.2 | convolution fusion | flops 807403520 | bytes 11927552 | tf_op jit(solution)/shard_map/dot_general | solution.py:81
  507.9 7.8 %pad_maximum_fusion = f32[2048,1024]{0,1:T(8,128)} fusion(f32[2048,512]{0,1:T(8,128)} %convolution_add_fusion, f32[2048,512]{0,1:T(8,128)} %convolution_add_fusion.1), kind=kLoop, calls=%fused_computation | loop fusion | flops 2097152 | bytes 16777216 | tf_op jit(solution)/shard_map/concatenate | solution.py:85
  515.7 9.2 %copy.7 = f32[2048,1024]{1,0:T(8,128)} copy(f32[2048,1024]{0,1:T(8,128)} %pad_maximum_fusion) | data formatting | bytes 16777216 | tf_op jit(solution)/shard_map/concatenate | solution.py:85
  (30 shorter events, 11.8 us)
Async XLA Ops:
  0.0 4.1 copy-start.2
  9.6 4.9 collective-permute-start.8
  14.4 4.2 collective-permute-start
  17.1 46.8 %collective-permute-start.9 = (f32[2048,256]{1,0:T(8,128)S(1)}, f32[2048,256]{1,0:T(8,128)S(1)}, u32[]{:S(2)}, u32[]{:S(2)}) collective-permute-start(f32[2048,256]{1,0:T(8,128)S(1)} %fusion.50), channel_id=1, source_target_pairs={{0,2},{1,3},{2,0},{3,1},{4,6},{5,7},{6,4},{7,5},{8,10},{9,11},{10,... | collective-permute-start | bytes 6291464 | tf_op jit(solution)/shard_map/ppermute | solution.py:28
  21.3 87.6 %collective-permute-start.1 = (f32[2048,256]{1,0:T(8,128)S(1)}, f32[2048,256]{1,0:T(8,128)S(1)}, u32[]{:S(2)}, u32[]{:S(2)}) collective-permute-start(f32[2048,256]{1,0:T(8,128)S(1)} %fusion.75), channel_id=1, source_target_pairs={{0,2},{1,3},{2,0},{3,1},{4,6},{5,7},{6,4},{7,5},{8,10},{9,11},{10,... | collective-permute-start | bytes 6291464 | tf_op jit(solution)/shard_map/ppermute | solution.py:28
  66.6 86.2 %collective-permute-start.10 = (f32[2048,256]{1,0:T(8,128)S(1)}, f32[2048,256]{1,0:T(8,128)S(1)}, u32[]{:S(2)}, u32[]{:S(2)}) collective-permute-start(f32[2048,256]{1,0:T(8,128)S(1)} %fusion.47), channel_id=1, source_target_pairs={{0,4},{1,5},{2,6},{3,7},{4,0},{5,1},{6,2},{7,3},{8,12},{9,13},{10,... | collective-permute-start | bytes 6291464 | tf_op jit(solution)/shard_map/ppermute | solution.py:28
  111.5 86.2 %collective-permute-start.2 = (f32[2048,256]{1,0:T(8,128)S(1)}, f32[2048,256]{1,0:T(8,128)S(1)}, u32[]{:S(2)}, u32[]{:S(2)}) collective-permute-start(f32[2048,256]{1,0:T(8,128)S(1)} %fusion.72), channel_id=1, source_target_pairs={{0,4},{1,5},{2,6},{3,7},{4,0},{5,1},{6,2},{7,3},{8,12},{9,13},{10,... | collective-permute-start | bytes 6291464 | tf_op jit(solution)/shard_map/ppermute | solution.py:28
  155.4 45.5 %collective-permute-start.11 = (f32[2048,256]{1,0:T(8,128)S(1)}, f32[2048,256]{1,0:T(8,128)S(1)}, u32[]{:S(2)}, u32[]{:S(2)}) collective-permute-start(f32[2048,256]{1,0:T(8,128)S(1)} %fusion.44), channel_id=1, source_target_pairs={{0,8},{1,9},{2,10},{3,11},{4,12},{5,13},{6,14},{7,15},{8,0},{9,1},... | collective-permute-start | bytes 6291464 | tf_op jit(solution)/shard_map/ppermute | solution.py:28
  200.4 46.1 %collective-permute-start.3 = (f32[2048,256]{1,0:T(8,128)S(1)}, f32[2048,256]{1,0:T(8,128)S(1)}, u32[]{:S(2)}, u32[]{:S(2)}) collective-permute-start(f32[2048,256]{1,0:T(8,128)S(1)} %fusion.69), channel_id=1, source_target_pairs={{0,8},{1,9},{2,10},{3,11},{4,12},{5,13},{6,14},{7,15},{8,0},{9,1},... | collective-permute-start | bytes 6291464 | tf_op jit(solution)/shard_map/ppermute | solution.py:28
  203.6 87.5 %collective-permute-start.12 = (f32[2048,256]{1,0:T(8,128)S(1)}, f32[2048,256]{1,0:T(8,128)S(1)}, u32[]{:S(2)}, u32[]{:S(2)}) collective-permute-start(f32[2048,256]{1,0:T(8,128)S(1)} %fusion.41), channel_id=1, source_target_pairs={{0,16},{1,17},{2,18},{3,19},{4,20},{5,21},{6,22},{7,23},{8,24},{9,... | collective-permute-start | bytes 6291464 | tf_op jit(solution)/shard_map/ppermute | solution.py:28
  249.2 86.9 %collective-permute-start.4 = (f32[2048,256]{1,0:T(8,128)S(1)}, f32[2048,256]{1,0:T(8,128)S(1)}, u32[]{:S(2)}, u32[]{:S(2)}) collective-permute-start(f32[2048,256]{1,0:T(8,128)S(1)} %fusion.66), channel_id=1, source_target_pairs={{0,16},{1,17},{2,18},{3,19},{4,20},{5,21},{6,22},{7,23},{8,24},{9,... | collective-permute-start | bytes 6291464 | tf_op jit(solution)/shard_map/ppermute | solution.py:28
  293.8 45.5 %collective-permute-start.13 = (f32[2048,256]{1,0:T(8,128)S(1)}, f32[2048,256]{1,0:T(8,128)S(1)}, u32[]{:S(2)}, u32[]{:S(2)}) collective-permute-start(f32[2048,256]{1,0:T(8,128)S(1)} %fusion.38), channel_id=1, source_target_pairs={{0,32},{1,33},{2,34},{3,35},{4,36},{5,37},{6,38},{7,39},{8,40},{9,... | collective-permute-start | bytes 6291464 | tf_op jit(solution)/shard_map/ppermute | solution.py:28
  338.7 45.3 %collective-permute-start.5 = (f32[2048,256]{1,0:T(8,128)S(1)}, f32[2048,256]{1,0:T(8,128)S(1)}, u32[]{:S(2)}, u32[]{:S(2)}) collective-permute-start(f32[2048,256]{1,0:T(8,128)S(1)} %fusion.63), channel_id=1, source_target_pairs={{0,32},{1,33},{2,34},{3,35},{4,36},{5,37},{6,38},{7,39},{8,40},{9,... | collective-permute-start | bytes 6291464 | tf_op jit(solution)/shard_map/ppermute | solution.py:28
  342.0 153.9 %collective-permute-start.14 = (f32[2048,256]{1,0:T(8,128)S(1)}, f32[2048,256]{1,0:T(8,128)}, u32[]{:S(2)}, u32[]{:S(2)}) collective-permute-start(f32[2048,256]{1,0:T(8,128)S(1)} %fusion.34), channel_id=1, source_target_pairs={{0,64},{1,65},{2,66},{3,67},{4,68},{5,69},{6,70},{7,71},{8,72},{9,... | collective-permute-start | bytes 6291464 | tf_op jit(solution)/shard_map/ppermute | solution.py:28
  385.3 102.7 %copy-start.1 = (bf16[2,768,512]{2,1,0:T(8,128)(2,1)S(1)}, bf16[2,768,512]{2,1,0:T(8,128)(2,1)}, u32[]{:S(2)}) copy-start(bf16[2,768,512]{2,1,0:T(8,128)(2,1)} %param.11) | copy-start | bytes 4718596
  388.2 113.7 %collective-permute-start.6 = (f32[2048,256]{1,0:T(8,128)}, f32[2048,256]{1,0:T(8,128)}, u32[]{:S(2)}, u32[]{:S(2)}) collective-permute-start(f32[2048,256]{1,0:T(8,128)} %fusion.59), channel_id=1, source_target_pairs={{0,64},{1,65},{2,66},{3,67},{4,68},{5,69},{6,70},{7,71},{8,72},{9,... | collective-permute-start | bytes 6291464 | tf_op jit(solution)/shard_map/ppermute | solution.py:28
  390.2 97.9 %collective-permute-start.15 = (bf16[2048,128]{1,0:T(8,128)(2,1)S(1)}, bf16[2048,128]{1,0:T(8,128)(2,1)S(1)}, u32[]{:S(2)}, u32[]{:S(2)}) collective-permute-start(bf16[2048,128]{1,0:T(8,128)(2,1)S(1)} %get-tuple-element.6), channel_id=1, source_target_pairs={{1,0},{2,1},{3,2},{4,3},{5,4},{6,5},{7,6},{8,7},{9,8},{10,9},{11,1... | collective-permute-start | bytes 1572872 | tf_op jit(solution)/shard_map/ppermute | solution.py:20
  397.7 94.2 %collective-permute-start.7 = (bf16[2048,128]{1,0:T(8,128)(2,1)S(1)}, bf16[2048,128]{1,0:T(8,128)(2,1)S(1)}, u32[]{:S(2)}, u32[]{:S(2)}) collective-permute-start(bf16[2048,128]{1,0:T(8,128)(2,1)S(1)} %get-tuple-element.5), channel_id=1, source_target_pairs={{0,1},{1,2},{2,3},{3,4},{4,5},{5,6},{6,7},{7,8},{8,9},{9,10},{10,1... | collective-permute-start | bytes 1572872 | tf_op jit(solution)/shard_map/ppermute | solution.py:18
  491.9 3.9 copy-start
where the time goes:
time: 526 us; the launch traced here: 525 us
  waiting for transfers between devices  416 us (79%)
  matrix products  62.8 us (12%)
  starting transfers between devices  24.7 us (5%)
  other arithmetic  11.9 us (2%)
  local copies, waits for them, and re-layouts  9.39 us (2%)
    ppermute x14, waiting for transfers between devices, from_partner(): lax.ppermute(shard, axis, [(i, i ^ 1 << apart) for i in range(lax.axis_si...  333 us
    ppermute x1, waiting for transfers between devices, with_halo(): lax.ppermute(head, axis, [((i + 1) % count, i) for i in range(ends)])  83.3 us
    dot_general x12, matrix products, per_device(): jnp.dot(proxies[which], stay_blocks[depth_at, which], preferred_element_t...  16 us
    dot_general x2, matrix products, per_device(): jnp.dot(proxies[which], out_basis[which], preferred_element_type=jnp.floa...  12 us
    dot_general x7, matrix products, per_device(): jnp.dot(proxies[0], cross_blocks[depth_at, 0], preferred_element_type=jnp...  10.8 us
  transfers between devices with their start and end apart: 16, of which 10 were waited for; matrix products, arithmetic and copies ran while one was open for 10% of the time, Pallas kernels for 0%

commit v1 on v0

v1 whole, which is shorter than its diff:
```python
import jax
import jax.numpy as jnp
from jax import lax
from jax.experimental import pallas as pl
from jax.experimental.pallas import tpu as pltpu
from jax.sharding import PartitionSpec as P

MESH = pl.DeviceIdType.MESH
BF = jnp.bfloat16
F32 = jnp.float32

B = 512
H = 128
R = 256
NV = 2048
CH = 256
NC = NV // CH
NU = 2 * NC
HALF = CH // 2
SLOTS = 4

T_ONE = 1
T_IN = (3, 9, 15)
T_MID = (5, 11, 17)
T_BACK = (7, 13, 19)
T_HALO = 16
STEPS = NU + T_BACK[2]
STRIDE = (2, 8, 32)


def mm(a, b):
    return jnp.dot(a, b, preferred_element_type=F32)


def kernel(
    src_h, leaf_h, stay_h, cross_h, outb_h, near_h, out_h,
    src_v, leaf_v, stay_v, cross_v, outb_v, near_v,
    pstay, pcross, win, xs1, xr1, pn, rsw, ab, xs, xr, bs, obuf,
    l_src, l_w, l_out,
    r_one, r_in, r_mid, r_back, r_halo, r_w,
    s_one, s_in, s_mid, s_back, s_halo, s_w,
):
    me = lax.axis_index("box")
    core = me % 2
    mate = me + 1 - 2 * core
    pos = [(me // st) % 4 for st in STRIDE]
    a_of = [me + (1 - 2 * (v % 2)) * st for v, st in zip(pos, STRIDE)]
    b_of = [me + (3 - 2 * v) * st for v, st in zip(pos, STRIDE)]
    half = [(v % 2 + v // 2) % 2 for v in pos]
    count = lax.axis_size("box")
    right = (me + 1) % count
    left = (me + count - 1) % count

    def local(src, dst, sem):
        return pltpu.make_async_copy(src, dst, sem)

    def remote(src, dst, ssem, rsem, to):
        return pltpu.make_async_remote_copy(
            src_ref=src, dst_ref=dst, send_sem=ssem, recv_sem=rsem,
            device_id=(to,), device_id_type=MESH,
        )

    def src_copy(c):
        return local(src_h.at[pl.ds(c * CH, CH)], src_v.at[c % SLOTS], l_src.at[c])

    loads = [
        local(h, v, l_w.at[i])
        for i, (h, v) in enumerate(
            ((leaf_h, leaf_v), (stay_h, stay_v), (cross_h, cross_v), (near_h, near_v), (outb_h, outb_v))
        )
    ]
    src_copy(0).start()
    loads[0].start()
    loads[1].start()
    loads[2].start()

    barrier = pltpu.get_barrier_semaphore()
    peers = [mate] + a_of + b_of + [left, right]
    for to in peers:
        pl.semaphore_signal(barrier, inc=1, device_id=(to,), device_id_type=MESH)
    pl.semaphore_wait(barrier, len(peers))

    def w_copy(d, which):
        level = 2 + 2 * d + which // 2
        held, there = ((stay_h, pstay), (cross_h, pcross))[which % 2]
        return remote(held.at[level], there.at[d, which // 2], s_w.at[d, which], r_w.at[d, which], a_of[d])

    for which in (0, 1, 3):
        w_copy(0, which).start()
    for d in (1, 2):
        for which in range(4):
            w_copy(d, which).start()
    for c in range(1, SLOTS):
        src_copy(c).start()
    loads[3].start()
    loads[4].start()

    @pl.when(me == 0)
    def _():
        for c in range(NC):
            win[c, :, 0:H] = jnp.zeros((CH, H), BF)

    @pl.when(me == count - 1)
    def _():
        for c in range(NC):
            win[c, :, H + 2 * B :] = jnp.zeros((CH, H), BF)

    for i in range(3):
        loads[i].wait()

    def one_copy(u):
        return remote(xs1.at[u], xr1.at[u], s_one, r_one.at[u], mate)

    def in_copy(d, u):
        return remote(pn.at[d, u, 1 - half[d]], rsw.at[d, u], s_in.at[d], r_in.at[d, u], a_of[d])

    def mid_copy(d, u):
        return remote(xs.at[d, u], xr.at[d, u], s_mid.at[d], r_mid.at[d, u], b_of[d])

    def back_copy(d, u, mine):
        at = half[d] if mine else 1 - half[d]
        return remote(bs.at[d, u], pn.at[d + 1, u, at], s_back.at[d], r_back.at[d, u], a_of[d])

    def halo_copy(side, c):
        if side == 0:
            return remote(
                win.at[c, :, pl.ds(2 * B, H)], win.at[c, :, pl.ds(0, H)], s_halo.at[0], r_halo.at[0, c], right
            )
        return remote(
            win.at[c, :, pl.ds(H, H)], win.at[c, :, pl.ds(H + 2 * B, H)], s_halo.at[1], r_halo.at[1, c], left
        )

    def out_copy(u):
        return local(
            obuf.at[u],
            out_h.at[pl.ds((u // 2) * CH, CH), pl.ds(pl.multiple_of((u % 2) * B, B), B)],
            l_out,
        )

    def leaf_stage(c):
        src_copy(c).wait()
        for h in range(2):
            rows = pl.ds(h * HALF, HALF)
            cells = src_v[c % SLOTS, rows, :].astype(BF)
            win[c, rows, H : H + 2 * B] = cells
            p0 = mm(cells[:, :B], leaf_v[0]).astype(BF)
            p1 = mm(cells[:, B:], leaf_v[1]).astype(BF)
            n0 = (mm(p0, stay_v[0, 0]) + mm(p1, cross_v[0, 1])).astype(BF)
            n1 = (mm(p1, stay_v[0, 1]) + mm(p0, cross_v[0, 0])).astype(BF)
            pn[0, 2 * c, h] = n0
            pn[0, 2 * c + 1, h] = n1
            xs1[2 * c, h] = mm(n0, cross_v[1, 0]).astype(BF)
            xs1[2 * c + 1, h] = mm(n1, cross_v[1, 1]).astype(BF)
        one_copy(2 * c).start()
        one_copy(2 * c + 1).start()

        @pl.when(c + SLOTS < NC)
        def _():
            src_copy(c + SLOTS).start()

    def one_stage(u):
        b = u % 2
        one_copy(u).wait_recv()
        for h in range(2):
            pn[0, u, h] = (mm(pn[0, u, h], stay_v[1, b]) + xr1[u, h].astype(F32)).astype(BF)
        in_copy(0, u).start()

        @pl.when(u == 0)
        def _():
            w_copy(0, 2).start()

    def in_stage(d, u):
        b = u % 2
        lev = 2 + 2 * d

        @pl.when(u == 0)
        def _():
            for which in (0, 1, 3):
                w_copy(d, which).wait_recv()

        in_copy(d, u).wait_recv()
        pa = pn[d, u, half[d]]
        pb = rsw[d, u]
        na = (mm(pa, stay_v[lev, b]) + mm(pb, pcross[d, 0, b])).astype(BF)
        nb = (mm(pb, pstay[d, 0, b]) + mm(pa, cross_v[lev, b])).astype(BF)
        xs[d, u, 0] = mm(na, cross_v[lev + 1, b]).astype(BF)
        xs[d, u, 1] = mm(nb, pcross[d, 1, b]).astype(BF)
        ab[d, u % 4, 0] = na
        ab[d, u % 4, 1] = nb
        mid_copy(d, u).start()

    def mid_stage(d, u):
        b = u % 2
        lev = 3 + 2 * d

        @pl.when(u == 0)
        def _():
            w_copy(d, 2).wait_recv()

        mid_copy(d, u).wait_recv()
        bs[d, u] = (mm(ab[d, u % 4, 1], pstay[d, 1, b]) + xr[d, u, 0].astype(F32)).astype(BF)
        back_copy(d, u, True).start()
        pn[d + 1, u, half[d]] = (mm(ab[d, u % 4, 0], stay_v[lev, b]) + xr[d, u, 1].astype(F32)).astype(BF)

    def back_stage(d, u):
        back_copy(d, u, False).wait_recv()
        if d < 2:
            in_copy(d + 1, u).start()

    def out_stage(u):
        b = u % 2
        c = u // 2

        @pl.when(u == 0)
        def _():
            loads[3].wait()
            loads[4].wait()

        @pl.when((b == 0) & (me > 0))
        def _():
            halo_copy(0, c).wait_recv()

        @pl.when((b == 1) & (me < count - 1))
        def _():
            halo_copy(1, c).wait_recv()

        cols = pl.ds(pl.multiple_of(b * B, B), B + 2 * H)
        for h in range(2):
            rows = pl.ds(h * HALF, HALF)
            total = mm(win[c, rows, cols], near_v[b]) + mm(pn[3, u, h], outb_v[b])
            obuf[u, rows, :] = total.astype(BF)
        out_copy(u).start()

    def step(t, _):
        def stage(at, body, count_of=NU):
            u = t - at

            @pl.when((u >= 0) & (u < count_of))
            def _():
                body(u)

        def finish(u):
            back_stage(2, u)
            out_stage(u)

        stage(T_BACK[2], finish)
        for d in (2, 1, 0):
            if d < 2:
                stage(T_BACK[d], lambda u, d=d: back_stage(d, u))
            stage(T_MID[d], lambda u, d=d: mid_stage(d, u))
            stage(T_IN[d], lambda u, d=d: in_stage(d, u))
        stage(T_ONE, one_stage)

        @pl.when((t % 2 == 0) & (t < NU))
        def _():
            leaf_stage(t // 2)

        def halos(c):
            @pl.when(me < count - 1)
            def _():
                halo_copy(0, c).start()

            @pl.when(me > 0)
            def _():
                halo_copy(1, c).start()

        stage(T_HALO, halos, NC)
        return 0

    lax.fori_loop(0, STEPS, step, 0)

    local(obuf, obuf, l_out).wait()
    remote(xs1, xr1, s_one, r_one.at[0], mate).wait_send()
    for d in range(3):
        remote(rsw.at[d], rsw.at[d], s_in.at[d], r_in.at[d, 0], a_of[d]).wait_send()
        remote(xs.at[d], xr.at[d], s_mid.at[d], r_mid.at[d, 0], b_of[d]).wait_send()
        remote(bs.at[d], bs.at[d], s_back.at[d], r_back.at[d, 0], a_of[d]).wait_send()
        for which in range(4):
            w_copy(d, which).wait_send()
    whole = rsw.at[0, pl.ds(0, NC)]

    @pl.when(me < count - 1)
    def _():
        remote(whole, whole, s_halo.at[0], r_halo.at[0, 0], right).wait_send()

    @pl.when(me > 0)
    def _():
        remote(whole, whole, s_halo.at[1], r_halo.at[1, 0], left).wait_send()


def per_device(sources, leaf_basis, stay_blocks, cross_blocks, out_basis, near_blocks):
    dma = pltpu.SemaphoreType.DMA
    v = pltpu.VMEM
    scratch = [
        v((SLOTS, CH, 2 * B), F32),
        v(leaf_basis.shape, BF),
        v(stay_blocks.shape, BF),
        v(cross_blocks.shape, BF),
        v(out_basis.shape, BF),
        v(near_blocks.shape, BF),
        v((3, 2, 2, R, R), BF),
        v((3, 2, 2, R, R), BF),
        v((NC, CH, 2 * B + 2 * H), BF),
        v((NU, 2, HALF, R), BF),
        v((NU, 2, HALF, R), BF),
        v((4, NU, 2, HALF, R), BF),
        v((3, NU, HALF, R), BF),
        v((3, 4, 2, HALF, R), BF),
        v((3, NU, 2, HALF, R), BF),
        v((3, NU, 2, HALF, R), BF),
        v((3, NU, HALF, R), BF),
        v((NU, CH, B), BF),
        dma((NC,)), dma((5,)), dma,
        dma((NU,)), dma((3, NU)), dma((3, NU)), dma((3, NU)), dma((2, NC)), dma((3, 4)),
        dma, dma((3,)), dma((3,)), dma((3,)), dma((2,)), dma((3, 4)),
    ]
    out = pl.pallas_call(
        kernel,
        out_shape=jax.ShapeDtypeStruct((NV, 2 * B), BF),
        in_specs=[pl.BlockSpec(memory_space=pl.ANY)] * 6,
        out_specs=pl.BlockSpec(memory_space=pl.ANY),
        scratch_shapes=scratch,
        compiler_params=pltpu.CompilerParams(
            collective_id=0, has_side_effects=True, vmem_limit_bytes=66_900_000
        ),
    )(sources, leaf_basis, stay_blocks, cross_blocks, out_basis, near_blocks)
    return out.astype(F32)


def solution(mesh):
    in_specs = (
        P(None, "box"),
        P("box", None, None),
        P(None, "box", None, None),
        P(None, "box", None, None),
        P("box", None, None),
        P("box", None, None),
    )
    return jax.shard_map(
        per_device, mesh=mesh, in_specs=in_specs, out_specs=P(None, "box"), check_vma=False
    )
```

time: 526 us -> 134 us (0.25)
  the two profiles are of different devices: /device:TPU:123 before, /device:TPU:0 now
where the time goes in v1:
time: 134 us; the launch traced here: 133 us
  Pallas kernels  127 us (95%)
  other arithmetic  6.63 us (5%)
    pallas_call x1, Pallas kernels, per_device(): pl.pallas_call(kernel, out_shape=jax.ShapeDtypeStruct((NV, 2 * B), BF), i...  127 us
    convert_element_type x1, other arithmetic, per_device(): return out.astype(F32)  6.63 us

profile of v1, /device:TPU:0, one launch (start us, length us, event | category | flops | bytes accessed | tf_op | source)
XLA Modules:
  0.0 133.4 jit_solution(15011003070591280402)
XLA Ops:
  0.0 126.8 %shard_map.64 = bf16[2048,1024]{1,0:T(8,128)(2,1)} custom-call(f32[2048,1024]{1,0:T(8,128)} %src_h.1, bf16[2,512,256]{2,1,0:T(8,128)(2,1)} %leaf_h.1, bf16[8,2,256,256]{3,2,1,0:T(8,128)(2,1)} %stay_h.1, bf16[8,2,256,256]{3,2,1,0:T(8,128)(2,1)} %cross_h.1, bf16[2,256,512]{2,1,0:T(8,128)(2,1)} %outb_h.1, bf16[2,768,512]{2,1,0:T(8,128)(2,1)} %near_h.1), custom_call_target="tpu_custom_call" | custom-call | tf_op jit(solution)/shard_map/pallas_call | solution.py:317
  126.8 6.6 %convert_element_type.3 = f32[2048,1024]{1,0:T(8,128)} convert(bf16[2048,1024]{1,0:T(8,128)(2,1)} %shard_map.64) | non-fusion elementwise | flops 2097152 | bytes 12582912 | tf_op jit(solution)/shard_map/convert_element_type | solution.py:327

commit v2 on v1

v2 whole, which is shorter than its diff:
```python
import jax
import jax.numpy as jnp
from jax import lax
from jax.experimental import pallas as pl
from jax.experimental.pallas import tpu as pltpu
from jax.sharding import PartitionSpec as P

MESH = pl.DeviceIdType.MESH
BF = jnp.bfloat16
F32 = jnp.float32

B = 512
H = 128
R = 256
NV = 2048
CH = 256
NC = NV // CH
NU = 2 * NC
HALF = CH // 2
SLOTS = 4

STRIDE = (2, 8, 32)
AHEAD = 2
STAGES = (("in", 0), ("mid", 0), ("back", 0), ("in", 1), ("mid", 1), ("back", 1), ("in", 2), ("mid", 2), ("back", 2))
FIRST = 8
AT_A = (0, 2, 4, 5, 7, 9, 10, 12, 14)
AT_B = (0, 2, 4, 5, 7, 9, 10, 12, 14)
LAG_A = dict(zip(("in", "mid", "back"), (AT_A[0::3], AT_A[1::3], AT_A[2::3])))
LAG_B = dict(zip(("in", "mid", "back"), (AT_B[0::3], AT_B[1::3], AT_B[2::3])))
STEPS = NU + LAG_B["back"][2]
HALO_AT = NU + 1
OUT_AT = HALO_AT + 2
OUT_RATE = 3
PIECE_AT = (0, 1, 2, 3, 4, 5, 6, 6)
KEYS = 8
WROWS = 128


def mm(a, b):
    return jnp.dot(a, b, preferred_element_type=F32)


def kernel(
    src_h, leaf_h, stay_h, cross_h, outb_h, near_h, out_h,
    src_v, leaf_v, w0, wl, w1, w2, wo, win, xs1, xr1, st1, pn, rsw, st, xs, xr, bs, obuf,
    l_src, l_w, l_out,
    r_one, r_in, r_mid, r_back, r_halo, r_w,
    s_one, s_in, s_mid, s_back, s_halo, s_w,
):
    me = lax.axis_index("box")
    core = me % 2
    mate = me + 1 - 2 * core
    pos = [(me // st) % 4 for st in STRIDE]
    a_of = [me + (1 - 2 * (v % 2)) * st for v, st in zip(pos, STRIDE)]
    b_of = [me + (3 - 2 * v) * st for v, st in zip(pos, STRIDE)]
    half = [(v % 2 + v // 2) % 2 for v in pos]
    count = lax.axis_size("box")
    right = (me + 1) % count
    left = (me + count - 1) % count

    def local(src, dst, sem):
        return pltpu.make_async_copy(src, dst, sem)

    def remote(src, dst, ssem, rsem, to):
        return pltpu.make_async_remote_copy(
            src_ref=src, dst_ref=dst, send_sem=ssem, recv_sem=rsem,
            device_id=(to,), device_id_type=MESH,
        )

    def src_copy(c):
        return local(src_h.at[pl.ds(c * CH, CH)], src_v.at[c % SLOTS], l_src.at[c % SLOTS])

    lo, hi = pl.ds(0, R), pl.ds(R, R)
    loads = [[(leaf_h, leaf_v)]]
    loads += [[(stay_h.at[0, 0], w0.at[lo, lo]), (cross_h.at[0, 0], w0.at[lo, hi]),
               (cross_h.at[0, 1], w0.at[hi, lo]), (stay_h.at[0, 1], w0.at[hi, hi])]]
    loads += [[(cross_h.at[1], wl.at[:, :, lo]), (stay_h.at[1], wl.at[:, :, hi])]]
    loads += [[(held.at[2 + 2 * d], w1.at[d, :, lo, at]) for d in range(3) for held, at in ((stay_h, lo), (cross_h, hi))]]
    loads += [[(held.at[3 + 2 * d], w2.at[d, 0, :, :, at]) for d in range(3) for held, at in ((cross_h, lo), (stay_h, hi))]]
    loads += [[(near_h, wo.at[:, pl.ds(0, B + 2 * H)]), (outb_h, wo.at[:, pl.ds(B + 2 * H, R)])]]
    loaded = [leaf_v, w0, wl, w1.at[:, :, lo], w2.at[:, 0], wo]

    def load(i):
        for src, dst in loads[i]:
            local(src, dst, l_w.at[i]).start()

    def load_wait(i):
        local(loaded[i], loaded[i], l_w.at[i]).wait()

    src_copy(0).start()
    for i in range(3):
        load(i)

    barrier = pltpu.get_barrier_semaphore()
    peers = [mate] + a_of + b_of + [left, right]
    for to in peers:
        pl.semaphore_signal(barrier, inc=1, device_id=(to,), device_id_type=MESH)
    pl.semaphore_wait(barrier, len(peers))

    def w_copy(d, b, part):
        some = pl.ds((part % 2) * (R // 2), R // 2)
        there = pl.ds(R + (part % 2) * (R // 2), R // 2)
        src, dst = (
            (stay_h.at[2 + 2 * d, b, some], w1.at[d, b, there, hi]),
            (cross_h.at[2 + 2 * d, b, some], w1.at[d, b, there, lo]),
            (cross_h.at[3 + 2 * d, b, some], w2.at[d, 1, b, some, lo]),
            (stay_h.at[3 + 2 * d, b, some], w2.at[d, 1, b, some, hi]),
        )[part // 2]
        return remote(src, dst, s_w.at[d], r_w.at[d, b], a_of[d])

    for d in range(3):
        for part in range(8):
            w_copy(d, 0, part).start()
    for d in (1, 2):
        for part in range(8):
            w_copy(d, 1, part).start()
    for c in range(1, SLOTS):
        src_copy(c).start()
    for i in range(3, 6):
        load(i)

    @pl.when(me == 0)
    def _():
        for c in range(NC):
            win[c, :, 0:H] = jnp.zeros((CH, H), BF)

    @pl.when(me == count - 1)
    def _():
        for c in range(NC):
            win[c, :, H + 2 * B :] = jnp.zeros((CH, H), BF)

    for i in range(3):
        load_wait(i)

    def one_copy(u):
        return remote(xs1.at[u], xr1.at[u], s_one, r_one.at[u // NC, u % 4], mate)

    def in_copy(d, u):
        return remote(pn.at[d, u, 1 - half[d]], rsw.at[d, u], s_in.at[d], r_in.at[d, u % KEYS], a_of[d])

    def mid_copy(d, u):
        return remote(xs.at[d, u], xr.at[d, u], s_mid.at[d], r_mid.at[d, u % KEYS], b_of[d])

    def back_copy(d, u, mine):
        at = half[d] if mine else 1 - half[d]
        return remote(bs.at[d, u], pn.at[d + 1, u, at], s_back.at[d], r_back.at[d, u % KEYS], a_of[d])

    def halo_copy(side, c):
        if side == 0:
            return remote(
                win.at[c, :, pl.ds(2 * B, H)], win.at[c, :, pl.ds(0, H)], s_halo.at[0], r_halo.at[0, c // 4], right
            )
        return remote(
            win.at[c, :, pl.ds(H, H)], win.at[c, :, pl.ds(H + 2 * B, H)], s_halo.at[1], r_halo.at[1, c // 4], left
        )

    late = ((core == 1) & (pos[0] % 2 == 0), (core == 0) & (pos[0] % 2 == 1))

    def halo_send(c, when):
        for side, there in ((0, me < count - 1), (1, me > 0)):
            chosen = late[side] if when else jnp.logical_not(late[side])

            @pl.when(there & chosen)
            def _(side=side):
                halo_copy(side, c).start()

    def out_copy(u):
        return local(
            obuf.at[u],
            out_h.at[pl.ds((u % NC) * CH, CH), pl.ds(pl.multiple_of((u // NC) * B, B), B)],
            l_out,
        )

    def leaf_stage(c):
        src_copy(c).wait()
        for h in range(2):
            rows = pl.ds(h * HALF, HALF)
            cells = src_v[c % SLOTS, rows, :].astype(BF)
            win[c, rows, H : H + 2 * B] = cells
            p0 = mm(cells[:, :B], leaf_v[0]).astype(BF)
            p1 = mm(cells[:, B:], leaf_v[1]).astype(BF)
            n = mm(jnp.concatenate([p0, p1], axis=1), w0[...]).astype(BF)
            for b in range(2):
                y = mm(n[:, b * R : (b + 1) * R], wl[b])
                xs1[b * NC + c, h] = y[:, :R].astype(BF)
                st1[c % 2, b, h] = y[:, R:]
        one_copy(c).start()
        one_copy(NC + c).start()

        @pl.when(c + SLOTS < NC)
        def _():
            src_copy(c + SLOTS).start()

    def one_stage(c):
        for b in range(2):
            u = b * NC + c
            one_copy(u).wait_recv()
            for h in range(2):
                pn[0, u, h] = (st1[c % 2, b, h] + xr1[u, h].astype(F32)).astype(BF)

        halo_send(c, 0)

        @pl.when(c < AHEAD)
        def _():
            in_copy(0, c).start()

    def in_stage(d, u):
        b = u // NC

        @pl.when(u % NC == 0)
        def _():
            whole = w1.at[d, b]
            remote(whole, whole, s_w.at[d], r_w.at[d, b], a_of[d]).wait_recv()

        if d == 0:

            @pl.when(u + AHEAD < NU)
            def _():
                in_copy(0, u + AHEAD).start()

            for part in range(8):

                @pl.when(u == PIECE_AT[part])
                def _(part=part):
                    w_copy(0, 1, part).start()

        in_copy(d, u).wait_recv()
        pair = jnp.concatenate([pn[d, u, half[d]], rsw[d, u]], axis=1)
        n = mm(pair, w1[d, b]).astype(BF)
        ya = mm(n[:, :R], w2[d, 0, b])
        yb = mm(n[:, R:], w2[d, 1, b])
        xs[d, u, 0] = ya[:, :R].astype(BF)
        xs[d, u, 1] = yb[:, :R].astype(BF)
        mid_copy(d, u).start()
        st[d, u % 4, 0] = ya[:, R:]
        st[d, u % 4, 1] = yb[:, R:]

    def mid_stage(d, u):
        mid_copy(d, u).wait_recv()
        bs[d, u] = (st[d, u % 4, 1] + xr[d, u, 0].astype(F32)).astype(BF)
        back_copy(d, u, True).start()
        pn[d + 1, u, half[d]] = (st[d, u % 4, 0] + xr[d, u, 1].astype(F32)).astype(BF)

    def back_stage(d, u):
        back_copy(d, u, False).wait_recv()
        if d < 2:
            in_copy(d + 1, u).start()

    def out_stage(d, u):
        b = u // NC
        c = u % NC

        some = rsw.at[0, pl.ds(0, NC // 2)]

        @pl.when((u % 4 == 0) & (b == 0) & (me > 0))
        def _():
            remote(some, some, s_halo.at[0], r_halo.at[0, c // 4], right).wait_recv()

        @pl.when((u % 4 == 0) & (b == 1) & (me < count - 1))
        def _():
            remote(some, some, s_halo.at[1], r_halo.at[1, c // 4], left).wait_recv()

        cols = pl.ds(pl.multiple_of(b * B, B), B + 2 * H)
        for h in range(2):
            rows = pl.ds(h * HALF, HALF)
            both = jnp.concatenate([win[c, rows, cols], pn[3, u, h]], axis=1)
            obuf[u, rows, :] = mm(both, wo[b]).astype(BF)
        out_copy(u).start()

    def prologue(i, _):
        @pl.when(i < NC)
        def _():
            leaf_stage(i)

        @pl.when(i > 0)
        def _():
            one_stage(i - 1)

        return 0

    lax.fori_loop(0, NC + 1, prologue, 0)
    for i in range(3, 6):
        load_wait(i)

    bodies = {"in": in_stage, "mid": mid_stage, "back": back_stage}

    def step(t, _):
        for kind, d in STAGES:
            a, b = t - LAG_A[kind][d], t - LAG_B[kind][d]
            u = jnp.where(a < FIRST, a, b)

            @pl.when((a >= 0) & ((a < FIRST) | (b >= FIRST)) & (u < NU))
            def _(u=u, kind=kind, d=d):
                bodies[kind](d, u)

        def outs(t):
            a, b = t + 1 - LAG_A["back"][2], t + 1 - LAG_B["back"][2]
            came = jnp.where(a < FIRST, a, jnp.maximum(b, FIRST))
            return jnp.clip(jnp.minimum(came, OUT_RATE * (t - OUT_AT + 1)), 0, NU)

        def result(u, _):
            out_stage(2, u)
            return 0

        lax.fori_loop(outs(t - 1), outs(t), result, 0)

        @pl.when((t >= HALO_AT) & (t < HALO_AT + 2))
        def _():
            for k in range(4):
                halo_send(4 * (t - HALO_AT) + k, 1)

        return 0

    lax.fori_loop(0, STEPS, step, 0)

    local(obuf, obuf, l_out).wait()
    remote(xs1, xr1, s_one, r_one.at[0, 0], mate).wait_send()
    for d in range(3):
        remote(rsw.at[d], rsw.at[d], s_in.at[d], r_in.at[d, 0], a_of[d]).wait_send()
        remote(xs.at[d], xr.at[d], s_mid.at[d], r_mid.at[d, 0], b_of[d]).wait_send()
        remote(bs.at[d], bs.at[d], s_back.at[d], r_back.at[d, 0], a_of[d]).wait_send()
        remote(w1.at[d], w1.at[d], s_w.at[d], r_w.at[d, 0], a_of[d]).wait_send()
    whole = rsw.at[0, pl.ds(0, NC)]

    @pl.when(me < count - 1)
    def _():
        remote(whole, whole, s_halo.at[0], r_halo.at[0, 0], right).wait_send()

    @pl.when(me > 0)
    def _():
        remote(whole, whole, s_halo.at[1], r_halo.at[1, 0], left).wait_send()


def widen_kernel(x_h, o_h, x_v, o_v, l_in, l_out):
    parts = NV // WROWS

    def get(i):
        return pltpu.make_async_copy(x_h.at[pl.ds(i * WROWS, WROWS)], x_v.at[i], l_in.at[i])

    def put(i):
        return pltpu.make_async_copy(o_v.at[i], o_h.at[pl.ds(i * WROWS, WROWS)], l_out.at[i])

    for i in range(parts):
        get(i).start()
    for i in range(parts):
        get(i).wait()
        o_v[i] = x_v[i].astype(F32)
        put(i).start()
    for i in range(parts):
        put(i).wait()


def widen(x):
    parts = NV // WROWS
    spec = pl.BlockSpec(memory_space=pl.ANY)
    return pl.pallas_call(
        widen_kernel, in_specs=[spec], out_specs=spec,
        out_shape=jax.ShapeDtypeStruct((NV, 2 * B), F32),
        scratch_shapes=[
            pltpu.VMEM((parts, WROWS, 2 * B), BF), pltpu.VMEM((parts, WROWS, 2 * B), F32),
            pltpu.SemaphoreType.DMA((parts,)), pltpu.SemaphoreType.DMA((parts,)),
        ],
        compiler_params=pltpu.CompilerParams(vmem_limit_bytes=60_000_000),
    )(x)


def per_device(sources, leaf_basis, stay_blocks, cross_blocks, out_basis, near_blocks):
    dma = pltpu.SemaphoreType.DMA
    v = pltpu.VMEM
    scratch = [
        v((SLOTS, CH, 2 * B), F32),
        v(leaf_basis.shape, BF),
        v((2 * R, 2 * R), BF),
        v((2, R, 2 * R), BF),
        v((3, 2, 2 * R, 2 * R), BF),
        v((3, 2, 2, R, 2 * R), BF),
        v((2, B + 2 * H + R, B), BF),
        v((NC, CH, 2 * B + 2 * H), BF),
        v((NU, 2, HALF, R), BF),
        v((NU, 2, HALF, R), BF),
        v((2, 2, 2, HALF, R), F32),
        v((4, NU, 2, HALF, R), BF),
        v((3, NU, HALF, R), BF),
        v((3, 4, 2, HALF, R), F32),
        v((3, NU, 2, HALF, R), BF),
        v((3, NU, 2, HALF, R), BF),
        v((3, NU, HALF, R), BF),
        v((NU, CH, B), BF),
        dma((SLOTS,)), dma((6,)), dma,
        dma((2, 4)), dma((3, KEYS)), dma((3, KEYS)), dma((3, KEYS)), dma((2, 2)), dma((3, 2)),
        dma, dma((3,)), dma((3,)), dma((3,)), dma((2,)), dma((3,)),
    ]
    out = pl.pallas_call(
        kernel,
        out_shape=jax.ShapeDtypeStruct((NV, 2 * B), BF),
        in_specs=[pl.BlockSpec(memory_space=pl.ANY)] * 6,
        out_specs=pl.BlockSpec(memory_space=pl.ANY),
        scratch_shapes=scratch,
        compiler_params=pltpu.CompilerParams(
            collective_id=0, has_side_effects=True, vmem_limit_bytes=66_900_000
        ),
    )(sources, leaf_basis, stay_blocks, cross_blocks, out_basis, near_blocks)
    return widen(out)


def solution(mesh):
    in_specs = (
        P(None, "box"),
        P("box", None, None),
        P(None, "box", None, None),
        P(None, "box", None, None),
        P("box", None, None),
        P("box", None, None),
    )
    return jax.shard_map(
        per_device, mesh=mesh, in_specs=in_specs, out_specs=P(None, "box"), check_vma=False
    )
```

time: 134 us -> 117 us (0.87)
  Pallas kernels: 127 us -> 117 us
  other arithmetic: 6.63 us -> 0 us
    pallas_call x1, Pallas kernels: 127 us -> 112 us  [per_device(): pl.pallas_call(kernel, out_shape=jax.ShapeDtypeStruct((NV, 2 * B), BF), i...]
    convert_element_type x1 -> x0, other arithmetic: 6.63 us -> none  [per_device(): return out.astype(F32)]
    pallas_call x0 -> x1, Pallas kernels: none -> 4.54 us  [widen(): pl.pallas_call(widen_kernel, in_specs=[spec], out_specs=spec, out_shape=j...]
where the time goes in v2:
time: 117 us
  Pallas kernels  117 us (100%)
    pallas_call x1, Pallas kernels, per_device(): pl.pallas_call(kernel, out_shape=jax.ShapeDtypeStruct((NV, 2 * B), BF), i...  112 us
    pallas_call x1, Pallas kernels, widen(): pl.pallas_call(widen_kernel, in_specs=[spec], out_specs=spec, out_shape=j...  4.54 us

profile of v2, /device:TPU:0, one launch (start us, length us, event | category | flops | bytes accessed | tf_op | source)
XLA Modules:
  0.0 116.6 jit_solution(15144298416770330477)
XLA Ops:
  0.0 112.0 %shard_map.64.x_h = bf16[2048,1024]{1,0:T(8,128)(2,1)} custom-call(f32[2048,1024]{1,0:T(8,128)} %src_h.1, bf16[2,512,256]{2,1,0:T(8,128)(2,1)} %leaf_h.1, bf16[8,2,256,256]{3,2,1,0:T(8,128)(2,1)} %stay_h.1, bf16[8,2,256,256]{3,2,1,0:T(8,128)(2,1)} %cross_h.1, bf16[2,256,512]{2,1,0:T(8,128)(2,1)} %outb_h.1, bf16[2,768,512]{2,1,0:T(8,128)(2,1)} %near_h.1), custom_call_target="tpu_custom_call" | custom-call | tf_op jit(solution)/shard_map/pallas_call | solution.py:393
  112.0 4.5 %shard_map.65 = f32[2048,1024]{1,0:T(8,128)} custom-call(bf16[2048,1024]{1,0:T(8,128)(2,1)} %shard_map.64.x_h), custom_call_target="tpu_custom_call" | custom-call | tf_op jit(solution)/shard_map/pallas_call | solution.py:356

commit v3 on v2

--- a/solution.py
+++ b/solution.py
@@ -20,18 +20,21 @@
 SLOTS = 4
 
 STRIDE = (2, 8, 32)
-AHEAD = 2
+AHEAD = 3
+BEFORE = AHEAD + 1
 STAGES = (("in", 0), ("mid", 0), ("back", 0), ("in", 1), ("mid", 1), ("back", 1), ("in", 2), ("mid", 2), ("back", 2))
 FIRST = 8
 AT_A = (0, 2, 4, 5, 7, 9, 10, 12, 14)
 AT_B = (0, 2, 4, 5, 7, 9, 10, 12, 14)
 LAG_A = dict(zip(("in", "mid", "back"), (AT_A[0::3], AT_A[1::3], AT_A[2::3])))
 LAG_B = dict(zip(("in", "mid", "back"), (AT_B[0::3], AT_B[1::3], AT_B[2::3])))
-STEPS = NU + LAG_B["back"][2]
+OUT_LAG = 1
+STEPS = NU + LAG_B["back"][2] + OUT_LAG
 HALO_AT = NU + 1
 OUT_AT = HALO_AT + 2
 OUT_RATE = 3
-PIECE_AT = (0, 1, 2, 3, 4, 5, 6, 6)
+PAIR_AT = 0
+PIECE_AT = (0, 0, 0, 0, 1, 1, 1, 1)
 KEYS = 8
 WROWS = 128
 
@@ -42,10 +45,10 @@
 
 def kernel(
     src_h, leaf_h, stay_h, cross_h, outb_h, near_h, out_h,
-    src_v, leaf_v, w0, wl, w1, w2, wo, win, xs1, xr1, st1, pn, rsw, st, xs, xr, bs, obuf,
+    src_v, leaf_v, w0, wl, w1, w2, wo, win, n1, xr1, pn, rsw, st, xs, xr, bs, fin, obuf,
     l_src, l_w, l_out,
-    r_one, r_in, r_mid, r_back, r_halo, r_w,
-    s_one, s_in, s_mid, s_back, s_halo, s_w,
+    r_one, r_in, r_mid, r_back, r_halo, r_w, r_pair, r_level, r_fin,
+    s_one, s_in, s_mid, s_back, s_halo, s_w, s_pair, s_level, s_pass, s_fin,
 ):
     me = lax.axis_index("box")
     core = me % 2
@@ -67,18 +70,22 @@
             device_id=(to,), device_id_type=MESH,
         )
 
-    def src_copy(c):
-        return local(src_h.at[pl.ds(c * CH, CH)], src_v.at[c % SLOTS], l_src.at[c % SLOTS])
-
+    def src_start(c):
+        for h in range(2):
+            rows = pl.ds(h * (NV // 2) + c * HALF, HALF)
+            local(src_h.at[rows], src_v.at[c % SLOTS, pl.ds(h * HALF, HALF)], l_src.at[c % SLOTS]).start()
+
+    def src_wait(c):
+        local(src_v.at[c % SLOTS], src_v.at[c % SLOTS], l_src.at[c % SLOTS]).wait()
+
+    keep = [core == h for h in half]
     lo, hi = pl.ds(0, R), pl.ds(R, R)
     loads = [[(leaf_h, leaf_v)]]
     loads += [[(stay_h.at[0, 0], w0.at[lo, lo]), (cross_h.at[0, 0], w0.at[lo, hi]),
                (cross_h.at[0, 1], w0.at[hi, lo]), (stay_h.at[0, 1], w0.at[hi, hi])]]
-    loads += [[(cross_h.at[1], wl.at[:, :, lo]), (stay_h.at[1], wl.at[:, :, hi])]]
-    loads += [[(held.at[2 + 2 * d], w1.at[d, :, lo, at]) for d in range(3) for held, at in ((stay_h, lo), (cross_h, hi))]]
-    loads += [[(held.at[3 + 2 * d], w2.at[d, 0, :, :, at]) for d in range(3) for held, at in ((cross_h, lo), (stay_h, hi))]]
+    loads += [[(stay_h.at[1], wl.at[:, lo, lo]), (cross_h.at[1], wl.at[:, lo, hi])]]
     loads += [[(near_h, wo.at[:, pl.ds(0, B + 2 * H)]), (outb_h, wo.at[:, pl.ds(B + 2 * H, R)])]]
-    loaded = [leaf_v, w0, wl, w1.at[:, :, lo], w2.at[:, 0], wo]
+    loaded = [leaf_v, w0, wl.at[:, lo], wo]
 
     def load(i):
         for src, dst in loads[i]:
@@ -87,17 +94,18 @@
     def load_wait(i):
         local(loaded[i], loaded[i], l_w.at[i]).wait()
 
-    src_copy(0).start()
+    src_start(0)
     for i in range(3):
         load(i)
 
     barrier = pltpu.get_barrier_semaphore()
-    peers = [mate] + a_of + b_of + [left, right]
+    other_of = [a + 1 - 2 * core for a in a_of]
+    peers = [mate] + a_of + other_of[1:] + b_of + [left, right]
     for to in peers:
         pl.semaphore_signal(barrier, inc=1, device_id=(to,), device_id_type=MESH)
     pl.semaphore_wait(barrier, len(peers))
 
-    def w_copy(d, b, part):
+    def w_copy(d, b, part, to):
         some = pl.ds((part % 2) * (R // 2), R // 2)
         there = pl.ds(R + (part % 2) * (R // 2), R // 2)
         src, dst = (
@@ -106,18 +114,63 @@
             (cross_h.at[3 + 2 * d, b, some], w2.at[d, 1, b, some, lo]),
             (stay_h.at[3 + 2 * d, b, some], w2.at[d, 1, b, some, hi]),
         )[part // 2]
-        return remote(src, dst, s_w.at[d], r_w.at[d, b], a_of[d])
-
-    for d in range(3):
+        return remote(src, dst, s_w.at[d], r_w.at[d, b], to)
+
+    def pair_blocks(d):
+        return (
+            (stay_h.at[2 + 2 * d], w1.at[d, :, lo, lo]),
+            (cross_h.at[2 + 2 * d], w1.at[d, :, lo, hi]),
+            (cross_h.at[3 + 2 * d], w2.at[d, 0, :, :, lo]),
+            (stay_h.at[3 + 2 * d], w2.at[d, 0, :, :, hi]),
+        )
+
+    def pass_on(b):
+        for ref in (w1.at[0, b, hi], w2.at[0, 1, b]):
+            remote(ref, ref, s_pass, r_w.at[0, b], mate).start()
+
+    def w_wait(d, b):
+        whole = w1.at[d, b]
+        remote(whole, whole, s_w.at[d], r_w.at[d, b], mate).wait_recv()
+
+    @pl.when(jnp.logical_not(keep[0]))
+    def _():
         for part in range(8):
-            w_copy(d, 0, part).start()
+            w_copy(0, 0, part, a_of[0]).start()
+
+    for src, dst in ((stay_h.at[1], wl.at[:, hi, hi]), (cross_h.at[1], wl.at[:, hi, lo])):
+        remote(src, dst, s_level, r_level, mate).start()
+    def pair_start(d):
+        @pl.when(keep[d])
+        def _():
+            for src, dst in pair_blocks(d):
+                local(src, dst, l_w.at[4 + d]).start()
+                remote(src, dst, s_pair.at[d], r_pair.at[d], mate).start()
+
+    def pair_wait(d):
+        @pl.when(keep[d])
+        def _():
+            local(w1.at[d], w1.at[d], l_w.at[4 + d]).wait()
+
+        @pl.when(jnp.logical_not(keep[d]))
+        def _():
+            remote(w1.at[d], w1.at[d], s_pair.at[d], r_pair.at[d], mate).wait_recv()
+
     for d in (1, 2):
-        for part in range(8):
-            w_copy(d, 1, part).start()
+
+        @pl.when(jnp.logical_not(keep[d]))
+        def _(d=d):
+            for to in (a_of[d], other_of[d]):
+                for src, dst in (
+                    (stay_h.at[2 + 2 * d], w1.at[d, :, hi, hi]),
+                    (cross_h.at[2 + 2 * d], w1.at[d, :, hi, lo]),
+                    (cross_h.at[3 + 2 * d], w2.at[d, 1, :, :, lo]),
+                    (stay_h.at[3 + 2 * d], w2.at[d, 1, :, :, hi]),
+                ):
+                    remote(src, dst, s_w.at[d], r_w.at[d, 0], to).start()
+
     for c in range(1, SLOTS):
-        src_copy(c).start()
-    for i in range(3, 6):
-        load(i)
+        src_start(c)
+    load(3)
 
     @pl.when(me == 0)
     def _():
@@ -131,9 +184,10 @@
 
     for i in range(3):
         load_wait(i)
+    remote(wl.at[:, hi], wl.at[:, hi], s_level, r_level, mate).wait_recv()
 
     def one_copy(u):
-        return remote(xs1.at[u], xr1.at[u], s_one, r_one.at[u // NC, u % 4], mate)
+        return remote(n1.at[u, 1 - core], xr1.at[u], s_one, r_one.at[u // NC, u % 4], mate)
 
     def in_copy(d, u):
         return remote(pn.at[d, u, 1 - half[d]], rsw.at[d, u], s_in.at[d], r_in.at[d, u % KEYS], a_of[d])
@@ -144,6 +198,9 @@
     def back_copy(d, u, mine):
         at = half[d] if mine else 1 - half[d]
         return remote(bs.at[d, u], pn.at[d + 1, u, at], s_back.at[d], r_back.at[d, u % KEYS], a_of[d])
+
+    def fin_copy(u):
+        return remote(pn.at[3, u, 1 - core], fin.at[u], s_fin, r_fin.at[u], mate)
 
     def halo_copy(side, c):
         if side == 0:
@@ -164,15 +221,13 @@
             def _(side=side):
                 halo_copy(side, c).start()
 
-    def out_copy(u):
-        return local(
-            obuf.at[u],
-            out_h.at[pl.ds((u % NC) * CH, CH), pl.ds(pl.multiple_of((u // NC) * B, B), B)],
-            l_out,
-        )
+    def out_copy(u, h):
+        rows = pl.ds(h * (NV // 2) + (u % NC) * HALF, HALF)
+        cols = pl.ds(pl.multiple_of((u // NC) * B, B), B)
+        return local(obuf.at[u, pl.ds(h * HALF, HALF)], out_h.at[rows, cols], l_out)
 
     def leaf_stage(c):
-        src_copy(c).wait()
+        src_wait(c)
         for h in range(2):
             rows = pl.ds(h * HALF, HALF)
             cells = src_v[c % SLOTS, rows, :].astype(BF)
@@ -180,49 +235,64 @@
             p0 = mm(cells[:, :B], leaf_v[0]).astype(BF)
             p1 = mm(cells[:, B:], leaf_v[1]).astype(BF)
             n = mm(jnp.concatenate([p0, p1], axis=1), w0[...]).astype(BF)
-            for b in range(2):
-                y = mm(n[:, b * R : (b + 1) * R], wl[b])
-                xs1[b * NC + c, h] = y[:, :R].astype(BF)
-                st1[c % 2, b, h] = y[:, R:]
+            n1[c, h] = n[:, :R]
+            n1[NC + c, h] = n[:, R:]
         one_copy(c).start()
         one_copy(NC + c).start()
 
         @pl.when(c + SLOTS < NC)
         def _():
-            src_copy(c + SLOTS).start()
+            src_start(c + SLOTS)
 
     def one_stage(c):
         for b in range(2):
             u = b * NC + c
             one_copy(u).wait_recv()
-            for h in range(2):
-                pn[0, u, h] = (st1[c % 2, b, h] + xr1[u, h].astype(F32)).astype(BF)
+            pair = jnp.concatenate([n1[u, core], xr1[u]], axis=1)
+            p = mm(pair, wl[b]).astype(BF)
+            pn[0, u, core] = p[:, :R]
+            pn[0, u, 1 - core] = p[:, R:]
 
         halo_send(c, 0)
 
-        @pl.when(c < AHEAD)
-        def _():
-            in_copy(0, c).start()
+        in_copy(0, c).start()
 
     def in_stage(d, u):
         b = u // NC
 
-        @pl.when(u % NC == 0)
-        def _():
-            whole = w1.at[d, b]
-            remote(whole, whole, s_w.at[d], r_w.at[d, b], a_of[d]).wait_recv()
-
         if d == 0:
 
-            @pl.when(u + AHEAD < NU)
+            @pl.when((u % NC == 0) & jnp.logical_not(keep[0]))
+            def _():
+                w_wait(0, b)
+
+            @pl.when(u == 2)
+            def _():
+                pair_start(2)
+
+            @pl.when((u == NC - 2) & keep[0])
+            def _():
+                w_wait(0, 1)
+                pass_on(1)
+
+        else:
+
+            @pl.when(u == 0)
+            def _():
+                pair_wait(d)
+                remote(w1.at[d], w1.at[d], s_w.at[d], r_w.at[d, 0], mate).wait_recv()
+
+        if d == 0:
+
+            @pl.when((u + AHEAD >= NC) & (u + AHEAD < NU))
             def _():
                 in_copy(0, u + AHEAD).start()
 
             for part in range(8):
 
-                @pl.when(u == PIECE_AT[part])
+                @pl.when((u == PIECE_AT[part]) & jnp.logical_not(keep[0]))
                 def _(part=part):
-                    w_copy(0, 1, part).start()
+                    w_copy(0, 1, part, a_of[0]).start()
 
         in_copy(d, u).wait_recv()
         pair = jnp.concatenate([pn[d, u, half[d]], rsw[d, u]], axis=1)
@@ -245,6 +315,8 @@
         back_copy(d, u, False).wait_recv()
         if d < 2:
             in_copy(d + 1, u).start()
+        else:
+            fin_copy(u).start()
 
     def out_stage(d, u):
         b = u // NC
@@ -260,31 +332,47 @@
         def _():
             remote(some, some, s_halo.at[1], r_halo.at[1, c // 4], left).wait_recv()
 
+        fin_copy(u).wait_recv()
         cols = pl.ds(pl.multiple_of(b * B, B), B + 2 * H)
+        for at, proxy in ((core, pn[3, u, core]), (1 - core, fin[u])):
+            rows = pl.ds(pl.multiple_of(at * HALF, HALF), HALF)
+            both = jnp.concatenate([win[c, rows, cols], proxy], axis=1)
+            obuf[u, rows, :] = mm(both, wo[b]).astype(BF)
         for h in range(2):
-            rows = pl.ds(h * HALF, HALF)
-            both = jnp.concatenate([win[c, rows, cols], pn[3, u, h]], axis=1)
-            obuf[u, rows, :] = mm(both, wo[b]).astype(BF)
-        out_copy(u).start()
+            out_copy(u, h).start()
+
+    def begin(i):
+        @pl.when(i < NC)
+        def _():
+            leaf_stage(i)
+
+            @pl.when(i == PAIR_AT)
+            def _():
+                pair_start(0)
+
+        @pl.when((i > 0) & (i <= NC))
+        def _():
+            one_stage(i - 1)
 
     def prologue(i, _):
-        @pl.when(i < NC)
-        def _():
-            leaf_stage(i)
-
-        @pl.when(i > 0)
-        def _():
-            one_stage(i - 1)
-
+        begin(i)
         return 0
 
-    lax.fori_loop(0, NC + 1, prologue, 0)
-    for i in range(3, 6):
-        load_wait(i)
+    lax.fori_loop(0, BEFORE, prologue, 0)
+    load_wait(3)
+    pair_wait(0)
+
+    @pl.when(keep[0])
+    def _():
+        w_wait(0, 0)
+        pass_on(0)
+
+    pair_start(1)
 
     bodies = {"in": in_stage, "mid": mid_stage, "back": back_stage}
 
     def step(t, _):
+        begin(t + BEFORE)
         for kind, d in STAGES:
             a, b = t - LAG_A[kind][d], t - LAG_B[kind][d]
             u = jnp.where(a < FIRST, a, b)
@@ -294,7 +382,7 @@
                 bodies[kind](d, u)
 
         def outs(t):
-            a, b = t + 1 - LAG_A["back"][2], t + 1 - LAG_B["back"][2]
+            a, b = t + 1 - OUT_LAG - LAG_A["back"][2], t + 1 - OUT_LAG - LAG_B["back"][2]
             came = jnp.where(a < FIRST, a, jnp.maximum(b, FIRST))
             return jnp.clip(jnp.minimum(came, OUT_RATE * (t - OUT_AT + 1)), 0, NU)
 
@@ -314,12 +402,27 @@
     lax.fori_loop(0, STEPS, step, 0)
 
     local(obuf, obuf, l_out).wait()
-    remote(xs1, xr1, s_one, r_one.at[0, 0], mate).wait_send()
+    remote(xr1, xr1, s_one, r_one.at[0, 0], mate).wait_send()
     for d in range(3):
         remote(rsw.at[d], rsw.at[d], s_in.at[d], r_in.at[d, 0], a_of[d]).wait_send()
         remote(xs.at[d], xr.at[d], s_mid.at[d], r_mid.at[d, 0], b_of[d]).wait_send()
         remote(bs.at[d], bs.at[d], s_back.at[d], r_back.at[d, 0], a_of[d]).wait_send()
-        remote(w1.at[d], w1.at[d], s_w.at[d], r_w.at[d, 0], a_of[d]).wait_send()
+        sent = w1.at[0] if d == 0 else w1.at[pl.ds(0, 2)]
+
+        @pl.when(keep[d])
+        def _(d=d):
+            remote(w1.at[d], w1.at[d], s_pair.at[d], r_pair.at[d], mate).wait_send()
+
+        @pl.when(jnp.logical_not(keep[d]))
+        def _(d=d, sent=sent):
+            remote(sent, sent, s_w.at[d], r_w.at[d, 0], a_of[d]).wait_send()
+
+    @pl.when(keep[0])
+    def _():
+        remote(w1.at[0], w1.at[0], s_pass, r_w.at[0, 0], mate).wait_send()
+
+    remote(wl.at[:, hi], wl.at[:, hi], s_level, r_level, mate).wait_send()
+    remote(fin, fin, s_fin, r_fin.at[0], mate).wait_send()
     whole = rsw.at[0, pl.ds(0, NC)]
 
     @pl.when(me < count - 1)
@@ -371,24 +474,24 @@
         v((SLOTS, CH, 2 * B), F32),
         v(leaf_basis.shape, BF),
         v((2 * R, 2 * R), BF),
-        v((2, R, 2 * R), BF),
+        v((2, 2 * R, 2 * R), BF),
         v((3, 2, 2 * R, 2 * R), BF),
         v((3, 2, 2, R, 2 * R), BF),
         v((2, B + 2 * H + R, B), BF),
         v((NC, CH, 2 * B + 2 * H), BF),
         v((NU, 2, HALF, R), BF),
-        v((NU, 2, HALF, R), BF),
-        v((2, 2, 2, HALF, R), F32),
+        v((NU, HALF, R), BF),
         v((4, NU, 2, HALF, R), BF),
         v((3, NU, HALF, R), BF),
         v((3, 4, 2, HALF, R), F32),
         v((3, NU, 2, HALF, R), BF),
         v((3, NU, 2, HALF, R), BF),
         v((3, NU, HALF, R), BF),
+        v((NU, HALF, R), BF),
         v((NU, CH, B), BF),
-        dma((SLOTS,)), dma((6,)), dma,
-        dma((2, 4)), dma((3, KEYS)), dma((3, KEYS)), dma((3, KEYS)), dma((2, 2)), dma((3, 2)),
-        dma, dma((3,)), dma((3,)), dma((3,)), dma((2,)), dma((3,)),
+        dma((SLOTS,)), dma((7,)), dma,
+        dma((2, 4)), dma((3, KEYS)), dma((3, KEYS)), dma((3, KEYS)), dma((2, 2)), dma((3, 2)), dma((3,)), dma, dma((NU,)),
+        dma, dma((3,)), dma((3,)), dma((3,)), dma((2,)), dma((3,)), dma((3,)), dma, dma, dma,
     ]
     out = pl.pallas_call(
         kernel,

time: 117 us -> 114 us (0.974)
  Pallas kernels: 117 us -> 113 us
    pallas_call x1, Pallas kernels: 112 us -> 108 us  [per_device(): pl.pallas_call(kernel, out_shape=jax.ShapeDtypeStruct((NV, 2 * B), BF), i...]
where the time goes in v3:
time: 114 us; the launch traced here: 113 us
  Pallas kernels  113 us (99%)
    pallas_call x1, Pallas kernels, per_device(): pl.pallas_call(kernel, out_shape=jax.ShapeDtypeStruct((NV, 2 * B), BF), i...  108 us
    pallas_call x1, Pallas kernels, widen(): pl.pallas_call(widen_kernel, in_specs=[spec], out_specs=spec, out_shape=j...  4.54 us

profile of v3, /device:TPU:0, one launch (start us, length us, event | category | flops | bytes accessed | tf_op | source)
XLA Modules:
  0.0 112.9 jit_solution(4145734666535561428)
XLA Ops:
  0.0 108.3 %shard_map.64.x_h = bf16[2048,1024]{1,0:T(8,128)(2,1)} custom-call(f32[2048,1024]{1,0:T(8,128)} %src_h.1, bf16[2,512,256]{2,1,0:T(8,128)(2,1)} %leaf_h.1, bf16[8,2,256,256]{3,2,1,0:T(8,128)(2,1)} %stay_h.1, bf16[8,2,256,256]{3,2,1,0:T(8,128)(2,1)} %cross_h.1, bf16[2,256,512]{2,1,0:T(8,128)(2,1)} %outb_h.1, bf16[2,768,512]{2,1,0:T(8,128)(2,1)} %near_h.1), custom_call_target="tpu_custom_call" | custom-call | tf_op jit(solution)/shard_map/pallas_call | solution.py:496
  108.3 4.5 %shard_map.65 = f32[2048,1024]{1,0:T(8,128)} custom-call(bf16[2048,1024]{1,0:T(8,128)(2,1)} %shard_map.64.x_h), custom_call_target="tpu_custom_call" | custom-call | tf_op jit(solution)/shard_map/pallas_call | solution.py:459

commit v4 on v3

--- a/solution.py
+++ b/solution.py
@@ -20,9 +20,9 @@
 SLOTS = 4
 
 STRIDE = (2, 8, 32)
-AHEAD = 3
+AHEAD = 2
 BEFORE = AHEAD + 1
-STAGES = (("in", 0), ("mid", 0), ("back", 0), ("in", 1), ("mid", 1), ("back", 1), ("in", 2), ("mid", 2), ("back", 2))
+STAGES = (("back", 0), ("back", 1), ("back", 2), ("in", 0), ("mid", 0), ("in", 1), ("mid", 1), ("in", 2), ("mid", 2))
 FIRST = 8
 AT_A = (0, 2, 4, 5, 7, 9, 10, 12, 14)
 AT_B = (0, 2, 4, 5, 7, 9, 10, 12, 14)
@@ -34,7 +34,7 @@
 OUT_AT = HALO_AT + 2
 OUT_RATE = 3
 PAIR_AT = 0
-PIECE_AT = (0, 0, 0, 0, 1, 1, 1, 1)
+PIECE_AT = (2, 2, 3, 3, 4, 4, 5, 5)
 KEYS = 8
 WROWS = 128
 

time: 114 us -> 113 us (level)
  Pallas kernels: 113 us -> 111 us
    pallas_call x1, Pallas kernels: 108 us -> 107 us  [per_device(): pl.pallas_call(kernel, out_shape=jax.ShapeDtypeStruct((NV, 2 * B), BF), i...]
where the time goes in v4:
time: 113 us; the launch traced here: 111 us
  Pallas kernels  111 us (98%)
    pallas_call x1, Pallas kernels, per_device(): pl.pallas_call(kernel, out_shape=jax.ShapeDtypeStruct((NV, 2 * B), BF), i...  107 us
    pallas_call x1, Pallas kernels, widen(): pl.pallas_call(widen_kernel, in_specs=[spec], out_specs=spec, out_shape=j...  4.54 us

profile of v4, /device:TPU:0, one launch (start us, length us, event | category | flops | bytes accessed | tf_op | source)
XLA Modules:
  0.0 111.1 jit_solution(8125733591847972545)
XLA Ops:
  0.0 106.6 %shard_map.64.x_h = bf16[2048,1024]{1,0:T(8,128)(2,1)} custom-call(f32[2048,1024]{1,0:T(8,128)} %src_h.1, bf16[2,512,256]{2,1,0:T(8,128)(2,1)} %leaf_h.1, bf16[8,2,256,256]{3,2,1,0:T(8,128)(2,1)} %stay_h.1, bf16[8,2,256,256]{3,2,1,0:T(8,128)(2,1)} %cross_h.1, bf16[2,256,512]{2,1,0:T(8,128)(2,1)} %outb_h.1, bf16[2,768,512]{2,1,0:T(8,128)(2,1)} %near_h.1), custom_call_target="tpu_custom_call" | custom-call | tf_op jit(solution)/shard_map/pallas_call | solution.py:496
  106.6 4.5 %shard_map.65 = f32[2048,1024]{1,0:T(8,128)} custom-call(bf16[2048,1024]{1,0:T(8,128)(2,1)} %shard_map.64.x_h), custom_call_target="tpu_custom_call" | custom-call | tf_op jit(solution)/shard_map/pallas_call | solution.py:459

commit v5 on v4

--- a/solution.py
+++ b/solution.py
@@ -35,7 +35,7 @@
 OUT_RATE = 3
 PAIR_AT = 0
 PIECE_AT = (2, 2, 3, 3, 4, 4, 5, 5)
-KEYS = 8
+KEYS = 6
 WROWS = 128
 
 

time: 113 us -> 113 us (level)
  no operation moved by 1% of the time
where the time goes in v5:
time: 113 us; the launch traced here: 111 us
  Pallas kernels  111 us (98%)
    pallas_call x1, Pallas kernels, per_device(): pl.pallas_call(kernel, out_shape=jax.ShapeDtypeStruct((NV, 2 * B), BF), i...  107 us
    pallas_call x1, Pallas kernels, widen(): pl.pallas_call(widen_kernel, in_specs=[spec], out_specs=spec, out_shape=j...  4.54 us

profile of v5, /device:TPU:0, one launch (start us, length us, event | category | flops | bytes accessed | tf_op | source)
XLA Modules:
  0.0 111.1 jit_solution(11754792849287613710)
XLA Ops:
  0.0 106.5 %shard_map.64.x_h = bf16[2048,1024]{1,0:T(8,128)(2,1)} custom-call(f32[2048,1024]{1,0:T(8,128)} %src_h.1, bf16[2,512,256]{2,1,0:T(8,128)(2,1)} %leaf_h.1, bf16[8,2,256,256]{3,2,1,0:T(8,128)(2,1)} %stay_h.1, bf16[8,2,256,256]{3,2,1,0:T(8,128)(2,1)} %cross_h.1, bf16[2,256,512]{2,1,0:T(8,128)(2,1)} %outb_h.1, bf16[2,768,512]{2,1,0:T(8,128)(2,1)} %near_h.1), custom_call_target="tpu_custom_call" | custom-call | tf_op jit(solution)/shard_map/pallas_call | solution.py:496
  106.5 4.5 %shard_map.65 = f32[2048,1024]{1,0:T(8,128)} custom-call(bf16[2048,1024]{1,0:T(8,128)(2,1)} %shard_map.64.x_h), custom_call_target="tpu_custom_call" | custom-call | tf_op jit(solution)/shard_map/pallas_call | solution.py:459
